TPU v7x, 128 devices: a whole 4x4x4 slice. The times are simulated.
128 devices in a mesh: tm: 16 (over y, z_lo, core), tensor: 8 (over z_hi, x).
Axes of the slice: x: 4, y: 4, z: 4 (z_hi: 2, z_lo: 2; z = z_hi * 2 + z_lo), core: 2. Of those that a mesh axis runs over, the one named last changes fastest.
Arguments:
- activations: bfloat16 [16384, 3072], P(('tm', 'tensor')), may hold values from -6 to 6
- mod_gain: float32 [3072], replicated, may hold values from 0.1 to 1.9
- mod_shift: float32 [3072], replicated, may hold values from -3 to 3
- out_gate: float32 [3072], replicated, may hold values from 0.5 to 2
- qkv_weight: bfloat16 [3072, 24, 384], P(None, 'tensor'), may hold values from -0.109375 to 0.109375
- out_weight: bfloat16 [24, 128, 3072], P('tensor'), may hold values from -0.109375 to 0.109375
- tile_mask: int32 [64, 7, 4, 4], P('tm'), may hold values 0 or 1
- cotangent: bfloat16 [16384, 3072], P('tm'), may hold values from -6 to 6
Outputs:
- layer_out: bfloat16 [16384, 3072], P(('tm', 'tensor'))
- input_grad: bfloat16 [16384, 3072], P(('tm', 'tensor'))
All inputs are finite; a program needn't handle non-finite values. No bound on the sum of `tile_mask` on one device may be relied on, other than what follows from the above.
Results may differ from a plain program's by a relative error of at most 0.015.
Values may be sent and summed in bfloat16 or wider, within the bound.
A program may use at most 320 MiB of HBM per device.

v0:
```python
import jax
import jax.numpy as jnp
from jax import lax
from jax.sharding import PartitionSpec as P

FRAME = 256
TILE = 64
RADIUS = 3
EPSILON = 1e-06


def extended(cells, sides, width):
    for axis, dim in sides:
        count = lax.axis_size(axis)
        ends = count - 1
        head = lax.slice_in_dim(cells, 0, width, axis=dim)
        tail = lax.slice_in_dim(cells, cells.shape[dim] - width, cells.shape[dim], axis=dim)
        cells = jnp.concatenate(
            [
                lax.ppermute(tail, axis, [(i, (i + 1) % count) for i in range(ends)]),
                cells,
                lax.ppermute(head, axis, [((i + 1) % count, i) for i in range(ends)]),
            ],
            axis=dim,
        )
    return cells


def norm_rows(inputs, mod_gain, mod_shift):
    floated = inputs.astype(jnp.float32)
    row_mean = jnp.mean(floated, axis=-1, keepdims=True)
    centered = floated - row_mean
    inverse = lax.rsqrt(jnp.mean(centered * centered, axis=-1, keepdims=True) + EPSILON)
    standard = centered * inverse
    return (standard, inverse, (standard * mod_gain + mod_shift).astype(jnp.bfloat16))


def norm_back(grad_norm, standard, inverse, mod_gain, cotangent):
    scaled_grad = grad_norm * mod_gain
    centered = scaled_grad - jnp.mean(scaled_grad, axis=-1, keepdims=True)
    projected = standard * jnp.mean(scaled_grad * standard, axis=-1, keepdims=True)
    return (cotangent.astype(jnp.float32) + inverse * (centered - projected)).astype(jnp.bfloat16)


def window_mask(tile_mask, first_frame, total_frames):
    expanded = jnp.repeat(jnp.repeat(tile_mask, TILE, axis=2), TILE, axis=3)
    frame_ids = lax.broadcasted_iota(jnp.int32, expanded.shape, 0) + first_frame
    offset_ids = lax.broadcasted_iota(jnp.int32, expanded.shape, 1)
    query_pos = lax.broadcasted_iota(jnp.int32, expanded.shape, 2)
    key_pos = lax.broadcasted_iota(jnp.int32, expanded.shape, 3)
    source = frame_ids + offset_ids - RADIUS
    diagonal = (offset_ids == RADIUS) & (query_pos // TILE == key_pos // TILE)
    inside = (source >= 0) & (source < total_frames)
    allowed = ((expanded == 1) | diagonal) & inside
    return jnp.transpose(allowed, (0, 2, 1, 3)).reshape(expanded.shape[0], expanded.shape[2], -1)


def window_rows(padded, frame_count, radius):
    stacked = jnp.stack(
        [padded[offset : offset + frame_count] for offset in range(2 * radius + 1)], axis=1
    )
    return stacked.reshape(frame_count, -1, padded.shape[2], padded.shape[3])


def spread_windows(window_grads, frame_count, radius):
    by_offset = window_grads.reshape(
        frame_count, 2 * radius + 1, -1, window_grads.shape[2], window_grads.shape[3]
    )
    summed = jnp.zeros((frame_count + 2 * radius,) + by_offset.shape[2:], jnp.float32)
    for offset in range(2 * radius + 1):
        summed = summed + jnp.pad(
            by_offset[:, offset], ((offset, 2 * radius - offset), (0, 0), (0, 0), (0, 0))
        )
    return summed


def attend(queries, window, allowed, score_scale):
    head_dim = queries.shape[-1]
    key_rows = window[..., :head_dim]
    value_rows = window[..., head_dim:]
    scores = (
        jnp.einsum("fqhc,fkhc->fhqk", queries, key_rows, preferred_element_type=jnp.float32)
        * score_scale
    )
    exponent = jnp.where(allowed[:, None], jnp.exp(scores), 0.0)
    totals = jnp.sum(exponent, axis=-1)
    numerator = jnp.einsum(
        "fhqk,fkhc->fqhc",
        exponent.astype(jnp.bfloat16),
        value_rows,
        preferred_element_type=jnp.float32,
    )
    output = (numerator / jnp.transpose(totals, (0, 2, 1))[..., None]).astype(jnp.bfloat16)
    return (output, totals)


def attend_back(queries, window, allowed, totals, output, grad_out, score_scale):
    head_dim = queries.shape[-1]
    key_rows = window[..., :head_dim]
    value_rows = window[..., head_dim:]
    scores = (
        jnp.einsum("fqhc,fkhc->fhqk", queries, key_rows, preferred_element_type=jnp.float32)
        * score_scale
    )
    probability = jnp.where(allowed[:, None], jnp.exp(scores), 0.0) / totals[..., None]
    grad_values = jnp.einsum(
        "fhqk,fqhc->fkhc",
        probability.astype(jnp.bfloat16),
        grad_out,
        preferred_element_type=jnp.float32,
    )
    grad_probs = jnp.einsum(
        "fqhc,fkhc->fhqk", grad_out, value_rows, preferred_element_type=jnp.float32
    )
    row_delta = jnp.einsum("fqhc,fqhc->fhq", grad_out, output, preferred_element_type=jnp.float32)
    grad_scores = (probability * (grad_probs - row_delta[..., None])).astype(jnp.bfloat16)
    grad_queries = jnp.einsum(
        "fhqk,fkhc->fqhc", grad_scores, key_rows, preferred_element_type=jnp.float32
    )
    grad_queries = (grad_queries * score_scale).astype(jnp.bfloat16)
    grad_keys = (
        jnp.einsum("fhqk,fqhc->fkhc", grad_scores, queries, preferred_element_type=jnp.float32)
        * score_scale
    )
    return (grad_queries, jnp.concatenate([grad_keys, grad_values], axis=-1))


def on_device(
    activations, mod_gain, mod_shift, out_gate, qkv_weight, out_weight, tile_mask, cotangent
):
    shard_rows = activations.shape[0]
    frame_count = tile_mask.shape[0]
    heads_here = qkv_weight.shape[1]
    head_dim = out_weight.shape[1]
    group_rows = frame_count * FRAME
    score_scale = head_dim ** (-0.5)
    standard, inverse, modulated = norm_rows(activations, mod_gain, mod_shift)
    joined_qkv = jnp.einsum(
        "rd,dhc->rhc",
        lax.all_gather(modulated, "tensor", axis=0, tiled=True),
        qkv_weight,
        preferred_element_type=jnp.float32,
    ).astype(jnp.bfloat16)
    joined_qkv = joined_qkv.reshape(frame_count, FRAME, heads_here, 3 * head_dim)
    queries = joined_qkv[..., :head_dim]
    padded = extended(joined_qkv[..., head_dim:], (("tm", 0),), RADIUS)
    first_frame = lax.axis_index("tm") * frame_count
    allowed = window_mask(tile_mask, first_frame, frame_count * lax.axis_size("tm"))
    window = window_rows(padded, frame_count, RADIUS)
    output, totals = attend(queries, window, allowed, score_scale)
    flat_out = output.reshape(group_rows, heads_here, head_dim)
    row_block = flat_out
    projection = lax.psum_scatter(
        jnp.einsum("rhc,hcd->rd", row_block, out_weight, preferred_element_type=jnp.float32).astype(
            jnp.bfloat16
        ),
        "tensor",
        scatter_dimension=0,
        tiled=True,
    ).astype(jnp.float32)
    layer_out = (activations.astype(jnp.float32) + out_gate * projection).astype(jnp.bfloat16)
    scaled = (cotangent.astype(jnp.float32) * out_gate).astype(jnp.bfloat16)
    grad_out = jnp.einsum("rd,hcd->rhc", scaled, out_weight, preferred_element_type=jnp.float32)
    grad_out = grad_out.astype(jnp.bfloat16).reshape(frame_count, FRAME, heads_here, head_dim)
    grad_queries, window_grads = attend_back(
        queries, window, allowed, totals, output, grad_out, score_scale
    )
    spread = spread_windows(window_grads, frame_count, RADIUS)
    rim_frames = jnp.concatenate([spread[:RADIUS], spread[frame_count + RADIUS :]], axis=0)
    arrived = extended(rim_frames.astype(jnp.bfloat16), (("tm", 0),), RADIUS).astype(
        rim_frames.dtype
    )
    own_part = spread[RADIUS : frame_count + RADIUS]
    from_below = jnp.pad(arrived[:RADIUS], ((0, frame_count - RADIUS), (0, 0), (0, 0), (0, 0)))
    from_above = jnp.pad(arrived[3 * RADIUS :], ((frame_count - RADIUS, 0), (0, 0), (0, 0), (0, 0)))
    grad_pairs = (own_part + from_below + from_above).astype(jnp.bfloat16)
    grad_joined = jnp.concatenate([grad_queries, grad_pairs], axis=-1).reshape(
        group_rows, heads_here, 3 * head_dim
    )
    row_block = grad_joined
    grad_norm = lax.psum_scatter(
        jnp.einsum("rhc,dhc->rd", row_block, qkv_weight, preferred_element_type=jnp.float32).astype(
            jnp.bfloat16
        ),
        "tensor",
        scatter_dimension=0,
        tiled=True,
    ).astype(jnp.float32)
    own_cotangent = lax.dynamic_slice_in_dim(
        cotangent, lax.axis_index("tensor") * shard_rows, shard_rows, 0
    )
    input_grad = norm_back(grad_norm, standard, inverse, mod_gain, own_cotangent)
    return (layer_out, input_grad)


def solution(mesh):
    placed = (
        P(("tm", "tensor"), None),
        P(),
        P(),
        P(),
        P(None, "tensor", None),
        P("tensor", None, None),
        P("tm", None, None, None),
        P("tm", None),
    )
    return jax.shard_map(
        on_device,
        mesh=mesh,
        in_specs=placed,
        out_specs=(P(("tm", "tensor"), None), P(("tm", "tensor"), None)),
        check_vma=False,
    )
```

profile of v0, /device:TPU:1, one launch (start us, length us, event | category | flops | bytes accessed | tf_op | source)
XLA Modules:
  0.0 538.4 jit_solution(2131804124469288829)
XLA Ops:
  14.4 91.4 %all-gather.2.cloned.1.call-done = bf16[1024,3072]{1,0:T(8,128)(2,1)} async-done(((bf16[128,3072]{1,0:T(8,128)(2,1)}), bf16[1024,3072]{1,0:T(8,128)(2,1)}) %all-gather.2.cloned.1.call-update) | async-done | bytes 6291472 | tf_op jit(solution)/shard_map/all_gather | solution.py:140
  105.8 12.4 %fusion.35 = bf16[1024,3,384]{2,0,1:T(8,128)(2,1)S(1)} fusion(bf16[3072,3,384]{2,0,1:T(8,128)(2,1)} %param.12, bf16[1024,3072]{1,0:T(8,128)(2,1)} %all-gather.2.cloned.1.call-done), kind=kOutput, calls=%fused_computation.60 | convolution fusion | flops 7248936960 | bytes 15728640 | tf_op jit(solution)/shard_map/rd,dhc->rhc/dot_general | solution.py:138
  123.5 6.3 %fusion.74 = bf16[1024,3,128]{2,0,1:T(8,128)(2,1)} fusion(bf16[3,128,3072]{2,1,0:T(8,128)(2,1)S(1)} %copy-done, bf16[1024,3072]{1,0:T(8,128)(2,1)} %param.15, f32[3072]{0:T(1024)S(1)} %copy-done.12), kind=kOutput, calls=%fused_computation.100 | convolution fusion | flops 2425749504 | bytes 9449472 | tf_op jit(solution)/shard_map/rd,hcd->rhc/dot_general | solution.py:163
  132.0 4.6 fusion.15
  136.5 5.5 %copy.27 = pred[4,256,1792]{2,1,0:T(8,128)(4,1)} copy(pred[4,256,1792]{1,2,0:T(8,128)(4,1)} %bitcast.112) | data formatting | bytes 3670016 | tf_op jit(solution)/shard_map/jit(_where)/broadcast_in_dim | solution.py:85
  146.1 3.5 collective-permute-done
  154.5 4.8 copy.25
  159.3 13.4 %fusion.1 = (f32[4,3,256]{2,1,0:T(4,128)S(1)}, f32[4,3,256,1792]{3,2,1,0:T(8,128)}) fusion(pred[4,256,1792]{2,1,0:T(8,128)(4,1)S(1)} %copy-done.6, bf16[4,1792,3,256]{3,1,2,0:T(8,128)(2,1)} %bitcast.108, bf16[4,256,3,384]{3,1,0,2:T(8,128)(2,1)S(1)} %bitcast.107), kind=kOutput, calls=%fused_computation.4 | convolution fusion | flops 1425798144 | bytes 30158848 | tf_op jit(solution)/shard_map/fqhc,fkhc->fhqk/dot_general | solution.py:82
  172.7 12.9 %fusion.22 = f32[4,1792,3,128]{1,3,2,0:T(8,128)} fusion(f32[4,3,256,1792]{3,2,1,0:T(8,128)} %get-tuple-element.20, f32[4,3,256]{2,1,0:T(4,128)S(1)} %get-tuple-element.19, pred[4,256,1792]{2,1,0:T(8,128)(4,1)S(1)} %copy-done.6, bf16[4,256,3,128]{3,1,0,2:T(8,128)(2,1)S(1)} %bitcast.116), kind=kOutput, calls=%fused_computation.30 | convolution fusion | flops 1431306240 | bytes 35663872 | tf_op jit(solution)/shard_map/fhqk,fqhc->fkhc/dot_general | solution.py:106
  185.6 13.6 %multiply_reduce_fusion = (f32[4,3,256]{2,1,0:T(4,128)S(1)}, bf16[4,256,3,128]{1,3,2,0:T(8,128)(2,1)}) fusion(f32[4,3,256,128]{2,3,1,0:T(8,128)} %copy.50, f32[4,256,3]{1,2,0:T(4,128)S(1)} %bitcast.120, f32[4,3,256,1792]{3,2,1,0:T(8,128)} %get-tuple-element.20, pred[4,256,1792]{2,1,0:T(8,128)(4,1)} %copy.27, bf16[4,1792,3,256]{3,1,2,0:T(8,128)(2,1)} %bitcast.109), kind=kOutput, calls=%fused_computation.96 | convolution fusion | flops 1427764224 | bytes 31744000 | tf_op jit(solution)/shard_map/fhqk,fkhc->fqhc/dot_general | solution.py:87
  199.2 17.3 %multiply_convert_fusion = bf16[4,3,256,1792]{3,2,1,0:T(8,128)(2,1)} fusion(f32[4,3,256]{2,1,0:T(4,128)S(1)} %get-tuple-element.21, bf16[4,1792,3,256]{3,1,2,0:T(8,128)(2,1)} %bitcast.110, f32[4,3,256]{2,1,0:T(4,128)S(1)} %get-tuple-element.19, f32[4,3,256,1792]{3,2,1,0:T(8,128)} %get-tuple-element.20, pred[4,256,1792]{2,1,0:T(8,128)(4,1)} %copy.27, ...), kind=kOutput, calls=%fused_computation.1 | convolution fusion | flops 1442316288 | bytes 41181184 | tf_op jit(solution)/shard_map/fqhc,fkhc->fhqk/dot_general | solution.py:112
  216.4 6.4 %multiply_bitcast_fusion = f32[4,1792,3,128]{1,3,2,0:T(8,128)S(1)} fusion(bf16[4,3,256,1792]{3,2,1,0:T(8,128)(2,1)} %multiply_convert_fusion, bf16[4,256,3,384]{3,1,0,2:T(8,128)(2,1)} %bitcast.105), kind=kOutput, calls=%fused_computation.12 | convolution fusion | flops 1412038656 | bytes 22806528 | tf_op jit(solution)/shard_map/fhqk,fqhc->fkhc/dot_general | solution.py:122
  223.9 7.7 %pad_maximum_fusion = f32[4,1792,3,256]{1,3,2,0:T(8,128)} fusion(f32[4,1792,3,128]{1,3,2,0:T(8,128)S(1)} %copy-done.4, f32[4,1792,3,128]{1,3,2,0:T(8,128)S(1)} %multiply_bitcast_fusion), kind=kLoop, calls=%fused_computation | loop fusion | flops 5505024 | bytes 44040192 | tf_op jit(solution)/shard_map/concatenate | solution.py:125
  231.6 21.7 %copy.35 = f32[4,1792,3,256]{3,1,2,0:T(8,128)} copy(f32[4,1792,3,256]{1,3,2,0:T(8,128)} %pad_maximum_fusion) | data formatting | bytes 44040192 | tf_op jit(solution)/shard_map/concatenate | solution.py:125
  253.3 14.5 %slice_bitcast_fusion.6 = (f32[4,256,3,256]{3,1,2,0:T(8,128)S(1)}, f32[4,256,3,256]{3,1,2,0:T(8,128)}, f32[4,256,3,256]{3,1,2,0:T(8,128)}, f32[4,256,3,256]{3,1,...) fusion(f32[4,7,256,3,256]{4,2,1,3,0:T(8,128)} %bitcast.102), kind=kLoop, calls=%fused_computation.51 | loop fusion | bytes 44040192 | tf_op jit(solution)/shard_map/squeeze | solution.py:72
  267.8 11.5 %fusion.91 = (bf16[10,256,3,256]{3,1,2,0:T(8,128)(2,1)}, f32[10,256,3,256]{3,1,2,0:T(8,128)}) fusion(f32[4,256,3,256]{3,1,2,0:T(8,128)} %get-tuple-element.11, f32[4,256,3,256]{3,1,2,0:T(8,128)} %get-tuple-element.12, f32[4,256,3,256]{3,1,2,0:T(8,128)} %get-tuple-element.7, f32[4,256,3,256]{3,1,2,0:T(8,128)} %get-tuple-element.8, ...), kind=kLoop, calls=%fused_computation.126 | loop fusion | flops 13762560 | bytes 33816576 | tf_op jit(solution)/shard_map/convert.2
  282.2 4.4 collective-permute-start.2
  288.5 10.4 %fusion.79 = bf16[4,256,3,128]{1,3,2,0:T(8,128)(2,1)} fusion(bf16[4,3,256,1792]{3,2,1,0:T(8,128)(2,1)} %multiply_convert_fusion, bf16[4,1792,3,256]{3,1,2,0:T(8,128)(2,1)} %bitcast.111), kind=kOutput, calls=%fused_computation.101 | convolution fusion | flops 1410072576 | bytes 17301504 | tf_op jit(solution)/shard_map/fhqk,fkhc->fqhc/dot_general | solution.py:117
  301.2 11.1 %collective-permute-done.2 = bf16[3,256,3,256]{3,1,2,0:T(8,128)(2,1)} collective-permute-done((bf16[3,256,3,256]{3,1,2,0:T(8,128)(2,1)S(1)}, bf16[3,256,3,256]{3,1,2,0:T(8,128)(2,1)}, u32[]{:S(2)}, u32[]{:S(2)}) %collective-permute-start.2) | collective-permute-done | bytes 1179680 | tf_op jit(solution)/shard_map/ppermute | solution.py:20
  317.7 10.1 %bitcast_convert_fusion = bf16[1024,3072]{1,0:T(8,128)(2,1)} fusion(bf16[1024,3,384]{2,0,1:T(8,128)(2,1)S(1)} %bitcast.113, bf16[3072,3,384]{2,0,1:T(8,128)(2,1)S(1)} %bitcast.119), kind=kOutput, calls=%fused_computation.6 | convolution fusion | flops 7250903040 | bytes 15728640 | tf_op jit(solution)/shard_map/rhc,dhc->rd/dot_general | solution.py:182
  330.1 6.6 %bitcast_convert_fusion.1 = bf16[1024,3072]{1,0:T(8,128)(2,1)} fusion(bf16[1024,3,128]{2,0,1:T(8,128)(2,1)} %bitcast.114, bf16[3,128,3072]{2,1,0:T(8,128)(2,1)S(1)} %copy-done), kind=kOutput, calls=%fused_computation.7 | convolution fusion | flops 2419064832 | bytes 9437184 | tf_op jit(solution)/shard_map/rhc,hcd->rd/dot_general | solution.py:154
  336.7 89.2 %reduce-scatter.5.cloned.1.call-done = bf16[128,3072]{1,0:T(8,128)(2,1)} async-done(((bf16[1024,3072]{1,0:T(8,128)(2,1)}), bf16[128,3072]{1,0:T(8,128)(2,1)}) %reduce-scatter.5.cloned.1.call-update) | async-done | bytes 786448 | tf_op jit(solution)/shard_map/reduce_scatter | solution.py:181
  427.6 100.6 %reduce-scatter.3.cloned.1.call-done = bf16[128,3072]{1,0:T(8,128)(2,1)} async-done(((bf16[1024,3072]{1,0:T(8,128)(2,1)}), bf16[128,3072]{1,0:T(8,128)(2,1)}) %reduce-scatter.3.cloned.1.call-update) | async-done | bytes 786448 | tf_op jit(solution)/shard_map/reduce_scatter | solution.py:153
  528.2 3.7 fusion.49
  (87 shorter events, 40.9 us)
Async XLA Ops:
  7.2 116.3 %copy-start = (bf16[3,128,3072]{2,1,0:T(8,128)(2,1)S(1)}, bf16[3,128,3072]{2,1,0:T(8,128)(2,1)}, u32[]{:S(2)}) copy-start(bf16[3,128,3072]{2,1,0:T(8,128)(2,1)} %param.13) | copy-start | bytes 7077892
  7.2 6.1 %copy-start.11 = (s32[4,7,4,4]{1,3,2,0:T(4,128)S(1)}, s32[4,7,4,4]{1,3,2,0:T(4,128)}, u32[]{:S(2)}) copy-start(s32[4,7,4,4]{1,3,2,0:T(4,128)} %param.14) | copy-start | bytes 5380
  7.2 98.6 %all-gather.2.cloned.1.call-start = ((), (), s32[]{:S(2)}) async-start(), calls=%async_computation.2 | async-start | bytes 7077888 | tf_op jit(solution)/shard_map/all_gather | solution.py:140
  13.2 412.8 %reduce-scatter.5.cloned.1.call-start = ((), (), s32[]{:S(2)}) async-start(), calls=%async_computation.4 | async-start | bytes 7077888 | tf_op jit(solution)/shard_map/reduce_scatter | solution.py:181
  118.3 11.5 %copy-start.2 = (bf16[1024,3,384]{2,0,1:T(8,128)(2,1)}, bf16[1024,3,384]{2,0,1:T(8,128)(2,1)S(1)}, u32[]{:S(2)}) copy-start(bf16[1024,3,384]{2,0,1:T(8,128)(2,1)S(1)} %fusion.35) | copy-start | bytes 7077892
  118.3 5.2 copy-start.12
  120.1 11.8 %copy-start.9 = (pred[4,7,256,4]{2,3,1,0:T(4,128)(4,1)S(1)}, pred[4,7,256,4]{2,3,1,0:T(4,128)(4,1)}, u32[]{:S(2)}) copy-start(pred[4,7,256,4]{2,3,1,0:T(4,128)(4,1)} %eq.23) | copy-start | bytes 86020
  120.1 29.5 %collective-permute-start = (bf16[3,256,3,256]{3,1,0,2:T(8,128)(2,1)}, bf16[3,256,3,256]{3,1,0,2:T(8,128)(2,1)}, u32[]{:S(2)}, u32[]{:S(2)}) collective-permute-start(bf16[3,256,3,256]{3,1,0,2:T(8,128)(2,1)} %get-tuple-element.16), channel_id=1, source_target_pairs={{0,8},{8,16},{16,24},{24,32},{32,40},{40,48},{48,56},{56,64},{64,7... | collective-permute-start | bytes 3538952 | tf_op jit(solution)/shard_map/ppermute | solution.py:20
  129.8 24.4 %collective-permute-start.1 = (bf16[3,256,3,256]{3,1,0,2:T(8,128)(2,1)}, bf16[3,256,3,256]{3,1,0,2:T(8,128)(2,1)S(1)}, u32[]{:S(2)}, u32[]{:S(2)}) collective-permute-start(bf16[3,256,3,256]{3,1,0,2:T(8,128)(2,1)} %get-tuple-element.15), channel_id=1, source_target_pairs={{8,0},{16,8},{24,16},{32,24},{40,32},{48,40},{56,48},{64,56},{72,6... | collective-permute-start | bytes 3538952 | tf_op jit(solution)/shard_map/ppermute | solution.py:22
  154.5 4.8 copy-start.6
  159.3 13.4 %copy-start.8 = (bf16[1024,3,128]{2,0,1:T(8,128)(2,1)S(1)}, bf16[1024,3,128]{2,0,1:T(8,128)(2,1)}, u32[]{:S(2)}) copy-start(bf16[1024,3,128]{2,0,1:T(8,128)(2,1)} %fusion.74) | copy-start | bytes 2359300
  216.4 7.5 %copy-start.4 = (f32[4,1792,3,128]{1,3,2,0:T(8,128)S(1)}, f32[4,1792,3,128]{1,3,2,0:T(8,128)}, u32[]{:S(2)}) copy-start(f32[4,1792,3,128]{1,3,2,0:T(8,128)} %fusion.22) | copy-start | bytes 33030148
  282.2 30.2 %collective-permute-start.2 = (bf16[3,256,3,256]{3,1,2,0:T(8,128)(2,1)S(1)}, bf16[3,256,3,256]{3,1,2,0:T(8,128)(2,1)}, u32[]{:S(2)}, u32[]{:S(2)}) collective-permute-start(bf16[3,256,3,256]{3,1,2,0:T(8,128)(2,1)S(1)} %get-tuple-element.13), channel_id=1, source_target_pairs={{0,8},{8,16},{16,24},{24,32},{32,40},{40,48},{48,56},{56,64},{64,7... | collective-permute-start | bytes 3538952 | tf_op jit(solution)/shard_map/ppermute | solution.py:20
  286.5 25.8 %collective-permute-start.3 = (bf16[3,256,3,256]{3,1,2,0:T(8,128)(2,1)}, bf16[3,256,3,256]{3,1,2,0:T(8,128)(2,1)}, u32[]{:S(2)}, u32[]{:S(2)}) collective-permute-start(bf16[3,256,3,256]{3,1,2,0:T(8,128)(2,1)} %get-tuple-element.14), channel_id=1, source_target_pairs={{8,0},{16,8},{24,16},{32,24},{40,32},{48,40},{56,48},{64,56},{72,6... | collective-permute-start | bytes 3538952 | tf_op jit(solution)/shard_map/ppermute | solution.py:22
  301.2 12.7 %copy-start.18 = (pred[4]{0:T(512)(128)(4,1)S(1)}, pred[4]{0:T(512)(128)(4,1)}, u32[]{:S(2)}) copy-start(pred[4]{0:T(512)(128)(4,1)} %constant.71.clone.1) | copy-start | bytes 16
  312.3 5.4 slice-start
  313.9 3.2 copy-start.5
  313.9 3.8 slice-start.1
  327.8 200.3 %reduce-scatter.3.cloned.1.call-start = ((), (), s32[]{:S(2)}) async-start(), calls=%async_computation.3 | async-start | bytes 7077888 | tf_op jit(solution)/shard_map/reduce_scatter | solution.py:153
  336.7 89.3 %copy-start.1 = (bf16[128,3072]{1,0:T(8,128)(2,1)S(1)}, bf16[128,3072]{1,0:T(8,128)(2,1)}, u32[]{:S(2)}) copy-start(bf16[128,3072]{1,0:T(8,128)(2,1)} %param.8) | copy-start | bytes 2359300
  336.7 89.3 %copy-start.10 = (f32[3072]{0:T(1024)S(1)}, f32[3072]{0:T(1024)}, u32[]{:S(2)}) copy-start(f32[3072]{0:T(1024)} %param.9) | copy-start | bytes 36868
  336.7 89.3 %copy-start.15 = (f32[128]{0:T(128)S(1)}, f32[128]{0:T(128)}, u32[]{:S(2)}) copy-start(f32[128]{0:T(128)} %copy-done.14) | copy-start | bytes 1540
  336.7 89.3 %copy-start.17 = (f32[128]{0:T(128)S(1)}, f32[128]{0:T(128)}, u32[]{:S(2)}) copy-start(f32[128]{0:T(128)} %copy-done.16) | copy-start | bytes 1540
  336.7 191.5 %copy-start.13 = (f32[3072]{0:T(1024)S(1)}, f32[3072]{0:T(1024)}, u32[]{:S(2)}) copy-start(f32[3072]{0:T(1024)} %param.11) | copy-start | bytes 36868
  (4 other events, 4.9 us)
Sparse Core Ops, SparseCore 0:
  13.3 92.4 all-gather.1
  328.0 97.9 reduce-scatter.4
  430.4 97.7 reduce-scatter.2
where the time goes:
time: 539 us; the launch traced here: 538 us
  waiting for transfers between devices  296 us (55%)
  matrix products  109 us (20%)
  local copies, waits for them, and re-layouts  63.4 us (12%)
  other arithmetic  43.8 us (8%)
  between operations  14.1 us (3%)
  starting transfers between devices  11.9 us (2%)
    reduce_scatter x1, waiting for transfers between devices, on_device(): lax.psum_scatter(jnp.einsum('rhc,hcd->rd', row_block, out_weight, preferr...  101 us
    all_gather x1, waiting for transfers between devices, on_device(): lax.all_gather(modulated, 'tensor', axis=0, tiled=True)  91.4 us
    reduce_scatter x1, waiting for transfers between devices, on_device(): lax.psum_scatter(jnp.einsum('rhc,dhc->rd', row_block, qkv_weight, preferr...  89.2 us
    concatenate x1, local copies, waits for them, and re-layouts, attend_back(): return (grad_queries, jnp.concatenate([grad_keys, grad_values], axis=-1))  21.7 us
    dot_general x1, matrix products, attend_back(): jnp.einsum('fqhc,fkhc->fhqk', grad_out, value_rows, preferred_element_typ...  17.3 us
    ppermute x2, waiting for transfers between devices, extended(): lax.ppermute(tail, axis, [(i, (i + 1) % count) for i in range(ends)])  14.6 us
    squeeze x1, local copies, waits for them, and re-layouts, spread_windows(): by_offset[:, offset]  14.5 us
    dot_general x1, matrix products, attend(): jnp.einsum('fhqk,fkhc->fqhc', exponent.astype(jnp.bfloat16), value_rows,...  13.6 us
  transfers between devices with their start and end apart: 7, of which 5 were waited for; matrix products, arithmetic and copies ran while one was open for 9% of the time, Pallas kernels for 0%

commit v1 on v0

--- a/solution.py
+++ b/solution.py
@@ -137,7 +137,9 @@
     standard, inverse, modulated = norm_rows(activations, mod_gain, mod_shift)
     joined_qkv = jnp.einsum(
         "rd,dhc->rhc",
-        lax.all_gather(modulated, "tensor", axis=0, tiled=True),
+        jnp.concatenate(
+            lax.all_to_all(jnp.stack([modulated] * lax.axis_size("tensor")), "tensor", 0, 0), axis=0
+        ),
         qkv_weight,
         preferred_element_type=jnp.float32,
     ).astype(jnp.bfloat16)

time: 539 us -> 556 us (1.032)
  starting transfers between devices: 11.9 us -> 20.1 us
    all_gather x1 -> x0, waiting for transfers between devices: 91.4 us -> none  [on_device(): lax.all_gather(modulated, 'tensor', axis=0, tiled=True)]
    all_to_all x0 -> x1, waiting for transfers between devices: none -> 72.3 us  [on_device(): lax.all_to_all(jnp.stack([modulated] * lax.axis_size('tensor')), 'tensor'...]
    reduce_scatter x1, waiting for transfers between devices: 89.2 us -> 113 us  [on_device(): lax.psum_scatter(jnp.einsum('rhc,dhc->rd', row_block, qkv_weight, preferr...]
    all_to_all x0 -> x1, starting transfers between devices: none -> 8.29 us  [on_device(): lax.all_to_all(jnp.stack([modulated] * lax.axis_size('tensor')), 'tensor'...]
where the time goes in v1:
time: 556 us; the launch traced here: 555 us
  waiting for transfers between devices  301 us (54%)
  matrix products  109 us (20%)
  local copies, waits for them, and re-layouts  66.9 us (12%)
  other arithmetic  43 us (8%)
  starting transfers between devices  20.1 us (4%)
  between operations  14.4 us (3%)
    reduce_scatter x1, waiting for transfers between devices, on_device(): lax.psum_scatter(jnp.einsum('rhc,dhc->rd', row_block, qkv_weight, preferr...  113 us
    reduce_scatter x1, waiting for transfers between devices, on_device(): lax.psum_scatter(jnp.einsum('rhc,hcd->rd', row_block, out_weight, preferr...  101 us
    all_to_all x1, waiting for transfers between devices, on_device(): lax.all_to_all(jnp.stack([modulated] * lax.axis_size('tensor')), 'tensor'...  72.3 us
    concatenate x1, local copies, waits for them, and re-layouts, attend_back(): return (grad_queries, jnp.concatenate([grad_keys, grad_values], axis=-1))  21.8 us
    dot_general x1, matrix products, attend_back(): jnp.einsum('fqhc,fkhc->fhqk', grad_out, value_rows, preferred_element_typ...  17.3 us
    ppermute x2, waiting for transfers between devices, extended(): lax.ppermute(tail, axis, [(i, (i + 1) % count) for i in range(ends)])  14.7 us
    squeeze x1, local copies, waits for them, and re-layouts, spread_windows(): by_offset[:, offset]  14.5 us
    dot_general x1, matrix products, attend(): jnp.einsum('fhqk,fkhc->fqhc', exponent.astype(jnp.bfloat16), value_rows,...  13.6 us
  transfers between devices with their start and end apart: 7, of which 5 were waited for; matrix products, arithmetic and copies ran while one was open for 9% of the time, Pallas kernels for 0%

profile of v1, /device:TPU:1, one launch (start us, length us, event | category | flops | bytes accessed | tf_op | source)
XLA Modules:
  0.0 554.7 jit_solution(9279968688472972569)
XLA Ops:
  15.7 8.3 %all-to-all-start = ((bf16[8,128,3072]{2,1,0:T(8,128)(2,1)}), bf16[8,128,3072]{2,1,0:T(8,128)(2,1)}, u32[]{:S(2)}, u32[]{:S(2)}) async-start(bf16[8,128,3072]{2,1,0:T(8,128)(2,1)} %stack.35), calls=%async_computation | async-start | bytes 12582912 | tf_op jit(solution)/shard_map/all_to_all | solution.py:141
  25.2 72.3 %all-to-all-done = bf16[8,128,3072]{2,1,0:T(8,128)(2,1)} async-done(((bf16[8,128,3072]{2,1,0:T(8,128)(2,1)}), bf16[8,128,3072]{2,1,0:T(8,128)(2,1)}, u32[]{:S(2)}, u32[]{:S(2)}) %all-to-all-start) | async-done | bytes 6291488 | tf_op jit(solution)/shard_map/all_to_all | solution.py:141
  97.5 12.4 %convolution_convert_fusion = bf16[1024,3,384]{2,0,1:T(8,128)(2,1)S(1)} fusion(bf16[1024,3072,1]{1,0,2:T(8,128)(2,1)} %bitcast.3, bf16[3072,3,384]{2,0,1:T(8,128)(2,1)} %param.12), kind=kOutput, calls=%fused_computation.58 | convolution fusion | flops 7248936960 | bytes 15728640 | tf_op jit(solution)/shard_map/rd,dhc->rhc/dot_general | solution.py:138
  115.4 6.3 %fusion.69 = bf16[1024,3,128]{2,0,1:T(8,128)(2,1)} fusion(bf16[3,128,3072]{2,1,0:T(8,128)(2,1)S(1)} %copy-done, bf16[1024,3072]{1,0:T(8,128)(2,1)} %param.15, f32[3072]{0:T(1024)S(1)} %copy-done.12), kind=kOutput, calls=%fused_computation.98 | convolution fusion | flops 2425749504 | bytes 9449472 | tf_op jit(solution)/shard_map/rd,hcd->rhc/dot_general | solution.py:165
  123.7 4.6 fusion.15
  128.3 5.4 copy.27
  146.4 4.8 copy.25
  151.2 13.3 %fusion.1 = (f32[4,3,256]{2,1,0:T(4,128)S(1)}, f32[4,3,256,1792]{3,2,1,0:T(8,128)}) fusion(pred[4,256,1792]{2,1,0:T(8,128)(4,1)S(1)} %copy-done.6, bf16[4,1792,3,256]{3,1,2,0:T(8,128)(2,1)} %bitcast.107, bf16[4,256,3,384]{3,1,0,2:T(8,128)(2,1)S(1)} %bitcast.106), kind=kOutput, calls=%fused_computation.4 | convolution fusion | flops 1425798144 | bytes 30158848 | tf_op jit(solution)/shard_map/fqhc,fkhc->fhqk/dot_general | solution.py:82
  164.5 12.9 %fusion.20 = f32[4,1792,3,128]{1,3,2,0:T(8,128)} fusion(f32[4,3,256,1792]{3,2,1,0:T(8,128)} %get-tuple-element.20, f32[4,3,256]{2,1,0:T(4,128)S(1)} %get-tuple-element.19, pred[4,256,1792]{2,1,0:T(8,128)(4,1)S(1)} %copy-done.6, bf16[4,256,3,128]{3,1,0,2:T(8,128)(2,1)S(1)} %bitcast.115), kind=kOutput, calls=%fused_computation.28 | convolution fusion | flops 1431306240 | bytes 35663872 | tf_op jit(solution)/shard_map/fhqk,fqhc->fkhc/dot_general | solution.py:106
  177.4 13.6 %multiply_reduce_fusion = (f32[4,3,256]{2,1,0:T(4,128)S(1)}, bf16[4,256,3,128]{1,3,2,0:T(8,128)(2,1)}) fusion(f32[4,3,256,128]{2,3,1,0:T(8,128)} %copy.50, f32[4,256,3]{1,2,0:T(4,128)S(1)} %bitcast.119, f32[4,3,256,1792]{3,2,1,0:T(8,128)} %get-tuple-element.20, pred[4,256,1792]{2,1,0:T(8,128)(4,1)} %copy.27, bf16[4,1792,3,256]{3,1,2,0:T(8,128)(2,1)} %bitcast.108), kind=kOutput, calls=%fused_computation.94 | convolution fusion | flops 1427764224 | bytes 31744000 | tf_op jit(solution)/shard_map/fhqk,fkhc->fqhc/dot_general | solution.py:87
  191.0 17.3 %multiply_convert_fusion = bf16[4,3,256,1792]{3,2,1,0:T(8,128)(2,1)} fusion(f32[4,3,256]{2,1,0:T(4,128)S(1)} %get-tuple-element.21, bf16[4,1792,3,256]{3,1,2,0:T(8,128)(2,1)} %bitcast.109, f32[4,3,256]{2,1,0:T(4,128)S(1)} %get-tuple-element.19, f32[4,3,256,1792]{3,2,1,0:T(8,128)} %get-tuple-element.20, pred[4,256,1792]{2,1,0:T(8,128)(4,1)} %copy.27, ...), kind=kOutput, calls=%fused_computation.1 | convolution fusion | flops 1442316288 | bytes 41181184 | tf_op jit(solution)/shard_map/fqhc,fkhc->fhqk/dot_general | solution.py:112
  208.3 6.4 %multiply_bitcast_fusion = f32[4,1792,3,128]{1,3,2,0:T(8,128)S(1)} fusion(bf16[4,3,256,1792]{3,2,1,0:T(8,128)(2,1)} %multiply_convert_fusion, bf16[4,256,3,384]{3,1,0,2:T(8,128)(2,1)} %bitcast.104), kind=kOutput, calls=%fused_computation.12 | convolution fusion | flops 1412038656 | bytes 22806528 | tf_op jit(solution)/shard_map/fhqk,fqhc->fkhc/dot_general | solution.py:122
  215.8 7.7 %pad_maximum_fusion = f32[4,1792,3,256]{1,3,2,0:T(8,128)} fusion(f32[4,1792,3,128]{1,3,2,0:T(8,128)S(1)} %copy-done.4, f32[4,1792,3,128]{1,3,2,0:T(8,128)S(1)} %multiply_bitcast_fusion), kind=kLoop, calls=%fused_computation | loop fusion | flops 5505024 | bytes 44040192 | tf_op jit(solution)/shard_map/concatenate | solution.py:125
  223.5 21.8 %copy.35 = f32[4,1792,3,256]{3,1,2,0:T(8,128)} copy(f32[4,1792,3,256]{1,3,2,0:T(8,128)} %pad_maximum_fusion) | data formatting | bytes 44040192 | tf_op jit(solution)/shard_map/concatenate | solution.py:125
  245.2 14.5 %slice_bitcast_fusion.6 = (f32[4,256,3,256]{3,1,2,0:T(8,128)S(1)}, f32[4,256,3,256]{3,1,2,0:T(8,128)}, f32[4,256,3,256]{3,1,2,0:T(8,128)}, f32[4,256,3,256]{3,1,...) fusion(f32[4,7,256,3,256]{4,2,1,3,0:T(8,128)} %bitcast.101), kind=kLoop, calls=%fused_computation.49 | loop fusion | bytes 44040192 | tf_op jit(solution)/shard_map/squeeze | solution.py:72
  259.7 11.5 %fusion.86 = (bf16[10,256,3,256]{3,1,2,0:T(8,128)(2,1)}, f32[10,256,3,256]{3,1,2,0:T(8,128)}) fusion(f32[4,256,3,256]{3,1,2,0:T(8,128)} %get-tuple-element.11, f32[4,256,3,256]{3,1,2,0:T(8,128)} %get-tuple-element.12, f32[4,256,3,256]{3,1,2,0:T(8,128)} %get-tuple-element.7, f32[4,256,3,256]{3,1,2,0:T(8,128)} %get-tuple-element.8, ...), kind=kLoop, calls=%fused_computation.124 | loop fusion | flops 13762560 | bytes 33816576 | tf_op jit(solution)/shard_map/convert.2
  274.1 4.4 collective-permute-start.2
  280.4 10.4 %fusion.74 = bf16[4,256,3,128]{1,3,2,0:T(8,128)(2,1)} fusion(bf16[4,3,256,1792]{3,2,1,0:T(8,128)(2,1)} %multiply_convert_fusion, bf16[4,1792,3,256]{3,1,2,0:T(8,128)(2,1)} %bitcast.110), kind=kOutput, calls=%fused_computation.99 | convolution fusion | flops 1410072576 | bytes 17301504 | tf_op jit(solution)/shard_map/fhqk,fkhc->fqhc/dot_general | solution.py:117
  293.1 11.1 %collective-permute-done.2 = bf16[3,256,3,256]{3,1,2,0:T(8,128)(2,1)} collective-permute-done((bf16[3,256,3,256]{3,1,2,0:T(8,128)(2,1)S(1)}, bf16[3,256,3,256]{3,1,2,0:T(8,128)(2,1)}, u32[]{:S(2)}, u32[]{:S(2)}) %collective-permute-start.2) | collective-permute-done | bytes 1179680 | tf_op jit(solution)/shard_map/ppermute | solution.py:20
  309.6 10.1 %bitcast_convert_fusion = bf16[1024,3072]{1,0:T(8,128)(2,1)} fusion(bf16[1024,3,384]{2,0,1:T(8,128)(2,1)S(1)} %bitcast.112, bf16[3072,3,384]{2,0,1:T(8,128)(2,1)S(1)} %bitcast.118), kind=kOutput, calls=%fused_computation.6 | convolution fusion | flops 7250903040 | bytes 15728640 | tf_op jit(solution)/shard_map/rhc,dhc->rd/dot_general | solution.py:184
  322.0 6.5 %bitcast_convert_fusion.1 = bf16[1024,3072]{1,0:T(8,128)(2,1)} fusion(bf16[1024,3,128]{2,0,1:T(8,128)(2,1)} %bitcast.113, bf16[3,128,3072]{2,1,0:T(8,128)(2,1)S(1)} %copy-done), kind=kOutput, calls=%fused_computation.7 | convolution fusion | flops 2419064832 | bytes 9437184 | tf_op jit(solution)/shard_map/rhc,hcd->rd/dot_general | solution.py:156
  328.6 112.8 %reduce-scatter.5.cloned.1.call-done = bf16[128,3072]{1,0:T(8,128)(2,1)} async-done(((bf16[1024,3072]{1,0:T(8,128)(2,1)}), bf16[128,3072]{1,0:T(8,128)(2,1)}) %reduce-scatter.5.cloned.1.call-update) | async-done | bytes 786448 | tf_op jit(solution)/shard_map/reduce_scatter | solution.py:183
  443.0 101.1 %reduce-scatter.3.cloned.1.call-done = bf16[128,3072]{1,0:T(8,128)(2,1)} async-done(((bf16[1024,3072]{1,0:T(8,128)(2,1)}), bf16[128,3072]{1,0:T(8,128)(2,1)}) %reduce-scatter.3.cloned.1.call-update) | async-done | bytes 786448 | tf_op jit(solution)/shard_map/reduce_scatter | solution.py:155
  544.2 3.7 fusion.44
  (87 shorter events, 47.0 us)
Async XLA Ops:
  7.2 108.2 %copy-start = (bf16[3,128,3072]{2,1,0:T(8,128)(2,1)S(1)}, bf16[3,128,3072]{2,1,0:T(8,128)(2,1)}, u32[]{:S(2)}) copy-start(bf16[3,128,3072]{2,1,0:T(8,128)(2,1)} %param.13) | copy-start | bytes 7077892
  15.7 8.3 %copy-start.11 = (s32[4,7,4,4]{1,3,2,0:T(4,128)S(1)}, s32[4,7,4,4]{1,3,2,0:T(4,128)}, u32[]{:S(2)}) copy-start(s32[4,7,4,4]{1,3,2,0:T(4,128)} %param.14) | copy-start | bytes 5380
  15.7 81.9 %all-to-all-start = ((bf16[8,128,3072]{2,1,0:T(8,128)(2,1)}), bf16[8,128,3072]{2,1,0:T(8,128)(2,1)}, u32[]{:S(2)}, u32[]{:S(2)}) async-start(bf16[8,128,3072]{2,1,0:T(8,128)(2,1)} %stack.35), calls=%async_computation | async-start | bytes 12582912 | tf_op jit(solution)/shard_map/all_to_all | solution.py:141
  23.9 417.4 %reduce-scatter.5.cloned.1.call-start = ((), (), s32[]{:S(2)}) async-start(), calls=%async_computation.4 | async-start | bytes 7077888 | tf_op jit(solution)/shard_map/reduce_scatter | solution.py:183
  110.0 11.7 %copy-start.2 = (bf16[1024,3,384]{2,0,1:T(8,128)(2,1)}, bf16[1024,3,384]{2,0,1:T(8,128)(2,1)S(1)}, u32[]{:S(2)}) copy-start(bf16[1024,3,384]{2,0,1:T(8,128)(2,1)S(1)} %convolution_convert_fusion) | copy-start | bytes 7077892
  110.0 5.4 copy-start.12
  111.9 11.8 %copy-start.9 = (pred[4,7,256,4]{2,3,1,0:T(4,128)(4,1)S(1)}, pred[4,7,256,4]{2,3,1,0:T(4,128)(4,1)}, u32[]{:S(2)}) copy-start(pred[4,7,256,4]{2,3,1,0:T(4,128)(4,1)} %eq.23) | copy-start | bytes 86020
  111.9 29.6 %collective-permute-start = (bf16[3,256,3,256]{3,1,0,2:T(8,128)(2,1)}, bf16[3,256,3,256]{3,1,0,2:T(8,128)(2,1)}, u32[]{:S(2)}, u32[]{:S(2)}) collective-permute-start(bf16[3,256,3,256]{3,1,0,2:T(8,128)(2,1)} %get-tuple-element.16), channel_id=1, source_target_pairs={{0,8},{8,16},{16,24},{24,32},{32,40},{40,48},{48,56},{56,64},{64,7... | collective-permute-start | bytes 3538952 | tf_op jit(solution)/shard_map/ppermute | solution.py:20
  121.7 24.4 %collective-permute-start.1 = (bf16[3,256,3,256]{3,1,0,2:T(8,128)(2,1)}, bf16[3,256,3,256]{3,1,0,2:T(8,128)(2,1)S(1)}, u32[]{:S(2)}, u32[]{:S(2)}) collective-permute-start(bf16[3,256,3,256]{3,1,0,2:T(8,128)(2,1)} %get-tuple-element.15), channel_id=1, source_target_pairs={{8,0},{16,8},{24,16},{32,24},{40,32},{48,40},{56,48},{64,56},{72,6... | collective-permute-start | bytes 3538952 | tf_op jit(solution)/shard_map/ppermute | solution.py:22
  146.4 4.8 copy-start.6
  151.2 13.3 %copy-start.8 = (bf16[1024,3,128]{2,0,1:T(8,128)(2,1)S(1)}, bf16[1024,3,128]{2,0,1:T(8,128)(2,1)}, u32[]{:S(2)}) copy-start(bf16[1024,3,128]{2,0,1:T(8,128)(2,1)} %fusion.69) | copy-start | bytes 2359300
  208.3 7.5 %copy-start.4 = (f32[4,1792,3,128]{1,3,2,0:T(8,128)S(1)}, f32[4,1792,3,128]{1,3,2,0:T(8,128)}, u32[]{:S(2)}) copy-start(f32[4,1792,3,128]{1,3,2,0:T(8,128)} %fusion.20) | copy-start | bytes 33030148
  274.1 30.2 %collective-permute-start.2 = (bf16[3,256,3,256]{3,1,2,0:T(8,128)(2,1)S(1)}, bf16[3,256,3,256]{3,1,2,0:T(8,128)(2,1)}, u32[]{:S(2)}, u32[]{:S(2)}) collective-permute-start(bf16[3,256,3,256]{3,1,2,0:T(8,128)(2,1)S(1)} %get-tuple-element.13), channel_id=1, source_target_pairs={{0,8},{8,16},{16,24},{24,32},{32,40},{40,48},{48,56},{56,64},{64,7... | collective-permute-start | bytes 3538952 | tf_op jit(solution)/shard_map/ppermute | solution.py:20
  278.5 25.8 %collective-permute-start.3 = (bf16[3,256,3,256]{3,1,2,0:T(8,128)(2,1)}, bf16[3,256,3,256]{3,1,2,0:T(8,128)(2,1)}, u32[]{:S(2)}, u32[]{:S(2)}) collective-permute-start(bf16[3,256,3,256]{3,1,2,0:T(8,128)(2,1)} %get-tuple-element.14), channel_id=1, source_target_pairs={{8,0},{16,8},{24,16},{32,24},{40,32},{48,40},{56,48},{64,56},{72,6... | collective-permute-start | bytes 3538952 | tf_op jit(solution)/shard_map/ppermute | solution.py:22
  293.1 12.7 %copy-start.18 = (pred[4]{0:T(512)(128)(4,1)S(1)}, pred[4]{0:T(512)(128)(4,1)}, u32[]{:S(2)}) copy-start(pred[4]{0:T(512)(128)(4,1)} %constant.71.clone.1) | copy-start | bytes 16
  304.2 5.4 slice-start
  305.8 3.2 copy-start.5
  305.8 3.8 slice-start.1
  319.8 224.4 %reduce-scatter.3.cloned.1.call-start = ((), (), s32[]{:S(2)}) async-start(), calls=%async_computation.3 | async-start | bytes 7077888 | tf_op jit(solution)/shard_map/reduce_scatter | solution.py:155
  328.5 112.8 %copy-start.1 = (bf16[128,3072]{1,0:T(8,128)(2,1)S(1)}, bf16[128,3072]{1,0:T(8,128)(2,1)}, u32[]{:S(2)}) copy-start(bf16[128,3072]{1,0:T(8,128)(2,1)} %param.8) | copy-start | bytes 2359300
  328.5 112.8 %copy-start.10 = (f32[3072]{0:T(1024)S(1)}, f32[3072]{0:T(1024)}, u32[]{:S(2)}) copy-start(f32[3072]{0:T(1024)} %param.9) | copy-start | bytes 36868
  328.5 112.9 %copy-start.15 = (f32[128]{0:T(128)S(1)}, f32[128]{0:T(128)}, u32[]{:S(2)}) copy-start(f32[128]{0:T(128)} %copy-done.14) | copy-start | bytes 1540
  328.5 112.9 %copy-start.17 = (f32[128]{0:T(128)S(1)}, f32[128]{0:T(128)}, u32[]{:S(2)}) copy-start(f32[128]{0:T(128)} %copy-done.16) | copy-start | bytes 1540
  328.5 215.6 %copy-start.13 = (f32[3072]{0:T(1024)S(1)}, f32[3072]{0:T(1024)}, u32[]{:S(2)}) copy-start(f32[3072]{0:T(1024)} %param.11) | copy-start | bytes 36868
  (4 other events, 5.0 us)
Sparse Core Ops, SparseCore 0:
  319.9 121.4 reduce-scatter.4
  445.8 98.3 reduce-scatter.2
